TPU v7x, 32 devices: a whole 2x2x4 slice. The times are simulated.
32 devices in a mesh: cell: 16 (over z, y, x), win: 2 (over core).
Axes of the slice: x: 2, y: 2, z: 4, core: 2. Of those that a mesh axis runs over, the one named last changes fastest.
Arguments:
- anomalies: bfloat16 [256, 60, 8192], P('win', None, 'cell'), may hold values from -6 to 6
- eofs: bfloat16 [100, 60, 8192], P('win', None, 'cell'), may hold values from -0.015625 to 0.015625
- cell_area: float32 [8192], P('cell'), may hold values from 0.5 to 2
- levels: int32 [8192], P('cell'), may hold values from 1 to 60
- counts: int32 [16], replicated, may hold values from 128 to 512, as said below
Outputs:
- pcs: float32 [256, 100], P('win')
- regression: float32 [100, 8192], P('win', 'cell')
Inputs may be any that keep to these rules, and one draw needn't show every extreme that they name: `counts`: every entry is at most 512, and some block holds exactly 512 real cells.
All inputs are finite; a program needn't handle non-finite values.
Results may differ from a plain program's by a relative error of at most 0.0049.
Values may be sent and summed in bfloat16 or wider, within the bound.
No kernel may reach another device: no remote copies, remote signals or barrier semaphores. Data moves between devices by JAX's collectives and lax.ppermute only.
A program may use at most 64 MiB of HBM per device.

v0:
```python
import jax
import jax.numpy as jnp
from jax import lax
from jax.sharding import PartitionSpec as P


def shards(anomalies, eofs, cell_area, levels, counts):
    steps_here, depth_count, slots = anomalies.shape
    position = lax.axis_index("cell")
    filled = counts[position]
    live = jnp.arange(slots, dtype=jnp.int32) < filled
    depth = jnp.arange(depth_count, dtype=jnp.int32)[:, None] < levels[None, :]
    mask = (live[None, :] & depth).astype(jnp.float32)
    weighted = (eofs.astype(jnp.float32) * (cell_area[None, :] * mask)[None]).astype(jnp.bfloat16)
    flat_data = anomalies.reshape(steps_here, depth_count * slots)
    piece = lax.all_gather(weighted, "win", axis=0, tiled=True)
    flat_piece = piece.reshape(piece.shape[0], depth_count * slots)
    partial_value = lax.dot_general(
        flat_data, flat_piece, (((1,), (1,)), ((), ())), preferred_element_type=jnp.float32
    )
    pcs = lax.psum(partial_value, "cell")
    column = jnp.sum(anomalies.astype(jnp.float32) * mask[None], axis=1).astype(jnp.bfloat16)
    pcs_rounded = pcs.astype(jnp.bfloat16)
    windows = lax.axis_size("win")
    term = lax.dot_general(
        pcs_rounded, column, (((0,), (0,)), ((), ())), preferred_element_type=jnp.float32
    )
    term = term / jnp.sqrt(jnp.float32(steps_here * windows))
    regression = lax.psum_scatter(term, "win", scatter_dimension=0, tiled=True)
    return (pcs, regression)


def solution(mesh):
    in_specs = (P("win", None, "cell"), P("win", None, "cell"), P("cell"), P("cell"), P())
    out_specs = (P("win", None), P("win", "cell"))
    return jax.shard_map(shards, mesh=mesh, in_specs=in_specs, out_specs=out_specs, check_vma=False)
```

profile of v0, /device:TPU:0, one launch (start us, length us, event | category | flops | bytes accessed | tf_op | source)
XLA Modules:
  0.0 138.4 jit_solution(9140950876646721835)
XLA Ops:
  7.2 0.0 copy-start.1
  7.2 0.0 all-gather.2.cloned.1.call-start
  7.2 1.2 dynamic_slice.3
  8.5 0.6 iota_compare_fusion.1
  9.1 0.7 fusion.9
  9.9 4.6 %multiply_convert_fusion = bf16[50,60,512]{2,1,0:T(8,128)(2,1)} fusion(bf16[50,60,512]{2,1,0:T(8,128)(2,1)} %param.6, f32[60,512]{1,0:T(8,128)S(1)} %fusion.9), kind=kLoop, calls=%fused_computation.1 | loop fusion | flops 4608000 | bytes 6266880 | tf_op jit(solution)/shard_map/convert_element_type | solution.py:14
  14.5 0.0 all-gather.2.cloned.1.call-update
  14.5 0.0 copy-done.1
  14.5 5.0 %multiply_reduce_fusion = bf16[128,512]{1,0:T(8,128)(2,1)S(1)} fusion(bf16[128,60,512]{2,0,1:T(8,128)(2,1)} %param.5, f32[60,512]{1,0:T(8,128)S(1)} %fusion.8), kind=kLoop, calls=%fused_computation | loop fusion | flops 11730944 | bytes 8118272 | tf_op jit(solution)/shard_map/reduce_sum | solution.py:22
  19.5 0.0 copy-start.2
  19.5 15.0 %all-gather.2.cloned.1.call-done = bf16[100,60,512]{2,1,0:T(8,128)(2,1)} async-done(((bf16[50,60,512]{2,1,0:T(8,128)(2,1)}), bf16[100,60,512]{2,1,0:T(8,128)(2,1)}) %all-gather.2.cloned.1.call-update) | async-done | bytes 6144016 | tf_op jit(solution)/shard_map/all_gather | solution.py:16
  34.5 12.3 %fusion.3 = f32[128,100]{0,1:T(8,128)S(1)} fusion(bf16[128,60,512]{2,0,1:T(8,128)(2,1)} %param.5, bf16[100,60,512]{2,1,0:T(8,128)(2,1)} %all-gather.2.cloned.1.call-done), kind=kOutput, calls=%fused_computation.5 | convolution fusion | flops 786432000 | bytes 14059520 | tf_op jit(solution)/shard_map/dot_general | solution.py:18
  46.8 77.1 %psum.7 = f32[128,100]{0,1:T(8,128)S(1)} all-reduce(f32[128,100]{0,1:T(8,128)S(1)} %fusion.3), channel_id=1, replica_groups=mesh['cell'=16,'win'=2] {'cell'}, use_global_device_ids=true, to_apply=%region_0.0 | all-reduce | flops 12800 | bytes 102400 | tf_op jit(solution)/shard_map/psum | solution.py:21
  123.9 0.0 copy-start
  123.9 0.2 convolution_multiply_fusion
  124.1 3.1 %fusion = f32[56,512]{1,0:T(8,128)S(1)} fusion(f32[100,512]{1,0:T(8,128)S(1)} %convolution_multiply_fusion), kind=kCustom, calls=%all-reduce-scatter | all-reduce-scatter fusion | flops 57345 | bytes 320000
  127.1 2.3 %collective-permute-start = (f32[6,512]{1,0:T(8,128)S(1)}, f32[6,512]{1,0:T(8,128)S(1)}, u32[]{:S(2)}, u32[]{:S(2)}) collective-permute-start(f32[6,512]{1,0:T(8,128)S(1)} %slice), channel_id=1, source_target_pairs={{0,1},{2,3},{4,5},{6,7},{8,9},{10,11},{12,13},{14,15},{16,17},{18,... | collective-permute-start | bytes 36872
  129.4 0.0 copy-done.2
  129.4 0.6 dynamic-slice.4
  130.7 0.0 collective-permute-done
  130.7 0.2 concatenate
  130.9 0.7 constant_dynamic-slice_fusion
  131.5 0.0 copy-done
  (2 shorter events, 0.0 us)
Async XLA Ops:
  7.2 7.3 %copy-start.1 = (s32[512]{0:T(512)S(1)}, s32[512]{0:T(512)}, u32[]{:S(2)}) copy-start(s32[512]{0:T(512)} %param.8) | copy-start | bytes 6148
  7.2 27.3 %all-gather.2.cloned.1.call-start = ((), (), s32[]{:S(2)}) async-start(), calls=%async_computation | async-start | bytes 9830400 | tf_op jit(solution)/shard_map/all_gather | solution.py:16
  19.5 109.9 %copy-start.2 = (u32[32]{0:T(128)S(1)}, u32[32]{0:T(128)}, u32[]{:S(2)}) copy-start(u32[32]{0:T(128)} %constant.18) | copy-start | bytes 388
  123.9 7.6 %copy-start = (f32[128,100]{0,1:T(8,128)}, f32[128,100]{0,1:T(8,128)S(1)}, u32[]{:S(2)}) copy-start(f32[128,100]{0,1:T(8,128)S(1)} %psum.7) | copy-start | bytes 153604
  127.1 3.5 %collective-permute-start = (f32[6,512]{1,0:T(8,128)S(1)}, f32[6,512]{1,0:T(8,128)S(1)}, u32[]{:S(2)}, u32[]{:S(2)}) collective-permute-start(f32[6,512]{1,0:T(8,128)S(1)} %slice), channel_id=1, source_target_pairs={{0,1},{2,3},{4,5},{6,7},{8,9},{10,11},{12,13},{14,15},{16,17},{18,... | collective-permute-start | bytes 36872
Sparse Core Ops, SparseCore 0:
  14.6 19.8 all-gather.1
where the time goes:
time: 139 us; the launch traced here: 138 us
  blocking collectives  80.2 us (58%)
  waiting for transfers between devices  15 us (11%)
  between operations  14.8 us (11%)
  matrix products  12.4 us (9%)
  other arithmetic  11 us (8%)
  local copies, waits for them, and re-layouts  2.69 us (2%)
  starting transfers between devices  2.3 us (2%)
    psum x1, blocking collectives, shards(): pcs = lax.psum(partial_value, 'cell')  77.1 us
    all_gather x1, waiting for transfers between devices, shards(): piece = lax.all_gather(weighted, 'win', axis=0, tiled=True)  15 us
    dot_general x1, matrix products, shards(): lax.dot_general(flat_data, flat_piece, (((1,), (1,)), ((), ())), preferre...  12.3 us
    reduce_sum x1, other arithmetic, shards(): jnp.sum(anomalies.astype(jnp.float32) * mask[None], axis=1)  5.01 us
    convert_element_type x1, other arithmetic, shards(): (eofs.astype(jnp.float32) * (cell_area[None, :] * mask)[None]).astype(jnp...  4.6 us
    unnamed x1, blocking collectives  3.06 us
  transfers between devices with their start and end apart: 2, of which 1 were waited for; matrix products, arithmetic and copies ran while one was open for 4% of the time, Pallas kernels for 0%

commit v1 on v0

--- a/solution.py
+++ b/solution.py
@@ -18,7 +18,7 @@
     partial_value = lax.dot_general(
         flat_data, flat_piece, (((1,), (1,)), ((), ())), preferred_element_type=jnp.float32
     )
-    pcs = lax.psum(partial_value, "cell")
+    pcs = jnp.sum(lax.all_gather(partial_value, "cell"), axis=0)
     column = jnp.sum(anomalies.astype(jnp.float32) * mask[None], axis=1).astype(jnp.bfloat16)
     pcs_rounded = pcs.astype(jnp.bfloat16)
     windows = lax.axis_size("win")

time: 139 us -> 108 us (0.78)
  blocking collectives: 80.2 us -> 48.8 us
    psum x1 -> x0, blocking collectives: 77.1 us -> none  [shards(): pcs = lax.psum(partial_value, 'cell')]
    all_gather x0 -> x1, blocking collectives: none -> 45.8 us  [shards(): pcs = jnp.sum(lax.all_gather(partial_value, 'cell'), axis=0)]
  transfers between devices with their start and end apart: 2 -> 2, of which waited for: 1 -> 1; matrix products, arithmetic and copies ran while one was open for 4% -> 5% of each run, Pallas kernels for 0% -> 0%
where the time goes in v1:
time: 108 us; the launch traced here: 107 us
  blocking collectives  48.8 us (45%)
  waiting for transfers between devices  15 us (14%)
  between operations  14.8 us (14%)
  matrix products  12.4 us (11%)
  other arithmetic  11.1 us (10%)
  local copies, waits for them, and re-layouts  2.84 us (3%)
  starting transfers between devices  2.3 us (2%)
    all_gather x1, blocking collectives, shards(): pcs = jnp.sum(lax.all_gather(partial_value, 'cell'), axis=0)  45.8 us
    all_gather x1, waiting for transfers between devices, shards(): piece = lax.all_gather(weighted, 'win', axis=0, tiled=True)  15 us
    dot_general x1, matrix products, shards(): lax.dot_general(flat_data, flat_piece, (((1,), (1,)), ((), ())), preferre...  12.3 us
    reduce_sum x1, other arithmetic, shards(): jnp.sum(anomalies.astype(jnp.float32) * mask[None], axis=1)  5.01 us
    convert_element_type x1, other arithmetic, shards(): (eofs.astype(jnp.float32) * (cell_area[None, :] * mask)[None]).astype(jnp...  4.6 us
    unnamed x1, blocking collectives  3.06 us
    unnamed x1, starting transfers between devices  2.26 us
  transfers between devices with their start and end apart: 2, of which 1 were waited for; matrix products, arithmetic and copies ran while one was open for 5% of the time, Pallas kernels for 0%

profile of v1, /device:TPU:0, one launch (start us, length us, event | category | flops | bytes accessed | tf_op | source)
XLA Modules:
  0.0 107.3 jit_solution(2913352738476523290)
XLA Ops:
  7.2 0.0 copy-start.1
  7.2 0.0 all-gather.3.cloned.1.call-start
  7.2 1.2 %dynamic_slice.3 = s32[1]{0:T(128)} dynamic-slice(s32[16]{0:T(128)} %param.9, s32[]{:T(128)S(6)} %select_n.3), dynamic_slice_sizes={1} | dynamic-slice | bytes 12 | tf_op jit(solution)/shard_map/dynamic_slice | solution.py:10
  8.5 0.6 iota_compare_fusion.1
  9.1 0.7 fusion.9
  9.9 4.6 %multiply_convert_fusion = bf16[50,60,512]{2,1,0:T(8,128)(2,1)} fusion(bf16[50,60,512]{2,1,0:T(8,128)(2,1)} %param.6, f32[60,512]{1,0:T(8,128)S(1)} %fusion.9), kind=kLoop, calls=%fused_computation.1 | loop fusion | flops 4608000 | bytes 6266880 | tf_op jit(solution)/shard_map/convert_element_type | solution.py:14
  14.5 0.0 all-gather.3.cloned.1.call-update
  14.5 0.0 copy-done.1
  14.5 5.0 %multiply_reduce_fusion = bf16[128,512]{1,0:T(8,128)(2,1)S(1)} fusion(bf16[128,60,512]{2,0,1:T(8,128)(2,1)} %param.5, f32[60,512]{1,0:T(8,128)S(1)} %fusion.8), kind=kLoop, calls=%fused_computation | loop fusion | flops 11730944 | bytes 8118272 | tf_op jit(solution)/shard_map/reduce_sum | solution.py:22
  19.5 0.0 copy-start.2
  19.5 15.0 %all-gather.3.cloned.1.call-done = bf16[100,60,512]{2,1,0:T(8,128)(2,1)} async-done(((bf16[50,60,512]{2,1,0:T(8,128)(2,1)}), bf16[100,60,512]{2,1,0:T(8,128)(2,1)}) %all-gather.3.cloned.1.call-update) | async-done | bytes 6144016 | tf_op jit(solution)/shard_map/all_gather | solution.py:16
  34.5 12.3 %fusion.3 = f32[128,100]{0,1:T(8,128)S(1)} fusion(bf16[128,60,512]{2,0,1:T(8,128)(2,1)} %param.5, bf16[100,60,512]{2,1,0:T(8,128)(2,1)} %all-gather.3.cloned.1.call-done), kind=kOutput, calls=%fused_computation.5 | convolution fusion | flops 786432000 | bytes 14059520 | tf_op jit(solution)/shard_map/dot_general | solution.py:18
  46.8 45.8 %all-gather = f32[2048,100]{0,1:T(8,128)S(1)} all-gather(f32[128,100]{0,1:T(8,128)S(1)} %fusion.3), channel_id=2, replica_groups=mesh['cell'=16,'win'=2] {'cell'}, dimensions={0}, use_global_device_ids=true | all-gather | bytes 870400 | tf_op jit(solution)/shard_map/all_gather | solution.py:21
  92.5 0.2 copy.9
  92.7 0.1 bitcast_reduce_fusion
  92.8 0.0 copy-start
  92.9 0.2 convolution_multiply_fusion
  93.0 3.1 %fusion = f32[56,512]{1,0:T(8,128)S(1)} fusion(f32[100,512]{1,0:T(8,128)S(1)} %convolution_multiply_fusion), kind=kCustom, calls=%all-reduce-scatter | all-reduce-scatter fusion | flops 57345 | bytes 320000
  96.1 2.3 %collective-permute-start = (f32[6,512]{1,0:T(8,128)S(1)}, f32[6,512]{1,0:T(8,128)S(1)}, u32[]{:S(2)}, u32[]{:S(2)}) collective-permute-start(f32[6,512]{1,0:T(8,128)S(1)} %slice), channel_id=1, source_target_pairs={{0,1},{2,3},{4,5},{6,7},{8,9},{10,11},{12,13},{14,15},{16,17},{18,... | collective-permute-start | bytes 36872
  98.4 0.6 dynamic-slice.4
  99.6 0.0 collective-permute-done
  99.6 0.2 concatenate
  99.8 0.7 constant_dynamic-slice_fusion
  100.5 0.0 copy-done
  (3 shorter events, 0.0 us)
Async XLA Ops:
  7.2 7.3 %copy-start.1 = (s32[512]{0:T(512)S(1)}, s32[512]{0:T(512)}, u32[]{:S(2)}) copy-start(s32[512]{0:T(512)} %param.8) | copy-start | bytes 6148
  7.2 27.3 %all-gather.3.cloned.1.call-start = ((), (), s32[]{:S(2)}) async-start(), calls=%async_computation | async-start | bytes 9830400 | tf_op jit(solution)/shard_map/all_gather | solution.py:16
  19.5 78.8 %copy-start.2 = (u32[32]{0:T(128)S(1)}, u32[32]{0:T(128)}, u32[]{:S(2)}) copy-start(u32[32]{0:T(128)} %constant.18) | copy-start | bytes 388
  92.8 7.6 %copy-start = (f32[128,100]{0,1:T(8,128)}, f32[128,100]{0,1:T(8,128)S(1)}, u32[]{:S(2)}) copy-start(f32[128,100]{0,1:T(8,128)S(1)} %bitcast_reduce_fusion) | copy-start | bytes 153604
  96.1 3.5 %collective-permute-start = (f32[6,512]{1,0:T(8,128)S(1)}, f32[6,512]{1,0:T(8,128)S(1)}, u32[]{:S(2)}, u32[]{:S(2)}) collective-permute-start(f32[6,512]{1,0:T(8,128)S(1)} %slice), channel_id=1, source_target_pairs={{0,1},{2,3},{4,5},{6,7},{8,9},{10,11},{12,13},{14,15},{16,17},{18,... | collective-permute-start | bytes 36872
Sparse Core Ops, SparseCore 0:
  14.6 19.8 all-gather.2
